TPU v7x, 256 devices: a whole 4x4x8 slice. The times are simulated.
256 devices in a mesh: row: 32 (over y, x, core), col: 8 (over z).
Axes of the slice: x: 4, y: 4, z: 8, core: 2. Of those that a mesh axis runs over, the one named last changes fastest.
Arguments:
- inputs: bfloat16 [768, 12288], P(None, 'col'), may hold values from -6 to 6
- out_grad: bfloat16 [768, 12288], P(None, 'col'), may hold values from -6 to 6
- pre_act: bfloat16 [768, 24576], P('col', 'row'), may hold values from -8 to 8
- w_in: bfloat16 [12288, 24576], P('col', 'row'), may hold values from -0.0546875 to 0.0546875
- w_out: bfloat16 [24576, 12288], P('row', 'col'), may hold values from -0.0390625 to 0.0390625
Outputs:
- grad_inputs: bfloat16 [768, 12288], P('row', 'col')
- grad_w_in: bfloat16 [12288, 24576], P('col', 'row')
- grad_w_out: bfloat16 [24576, 12288], P('row', 'col')
All inputs are finite; a program needn't handle non-finite values.
Results may differ from a plain program's by a relative error of at most 0.0049.
Values may be sent and summed in bfloat16 or wider, within the bound.
A program may use at most 64 MiB of HBM per device.

v0:
```python
import math
import jax
import jax.numpy as jnp
from jax import lax
from jax.sharding import PartitionSpec as P

coef_c = math.sqrt(2.0 / math.pi)


def gelu_parts(pre_values):
    hval = pre_values.astype(jnp.float32)
    tval = jnp.tanh(coef_c * (hval + 0.044715 * hval * hval * hval))
    activ = 0.5 * hval * (1.0 + tval)
    deriv = 0.5 * (1.0 + tval) + 0.5 * hval * (1.0 - tval * tval) * coef_c * (
        1.0 + 3.0 * 0.044715 * hval * hval
    )
    return (activ, deriv)


def per_device(inputs, out_grad, pre_act, w_in, w_out):
    total_tokens = inputs.shape[0]
    scale_value = 1.0 / math.sqrt(total_tokens)
    block = out_grad
    act_share = lax.psum_scatter(
        lax.dot_general(block, w_out, (((1,), (1,)), ((), ())), preferred_element_type=jnp.float32),
        "col",
        scatter_dimension=0,
        tiled=True,
    )
    local_act, local_deriv = gelu_parts(pre_act)
    hid_share = (act_share * local_deriv).astype(jnp.bfloat16)
    activ_all, hid_all = (
        lax.all_gather(local_act.astype(jnp.bfloat16), "col", axis=0, tiled=True),
        lax.all_gather(hid_share, "col", axis=0, tiled=True),
    )
    grad_w_out = lax.dot_general(
        activ_all, out_grad, (((0,), (0,)), ((), ())), preferred_element_type=jnp.float32
    )
    grad_w_out = (grad_w_out * scale_value).astype(jnp.bfloat16)
    grad_w_in = lax.dot_general(
        inputs, hid_all, (((0,), (0,)), ((), ())), preferred_element_type=jnp.float32
    )
    grad_w_in = (grad_w_in * scale_value).astype(jnp.bfloat16)
    block = hid_all
    grad_inputs = lax.psum_scatter(
        lax.dot_general(block, w_in, (((1,), (1,)), ((), ())), preferred_element_type=jnp.float32),
        "row",
        scatter_dimension=0,
        tiled=True,
    )
    return (grad_inputs.astype(jnp.bfloat16), grad_w_in, grad_w_out)


def solution(mesh):
    placed = (P(None, "col"), P(None, "col"), P("col", "row"), P("col", "row"), P("row", "col"))
    return jax.shard_map(
        per_device,
        mesh=mesh,
        in_specs=placed,
        out_specs=(P("row", "col"), P("col", "row"), P("row", "col")),
        check_vma=False,
    )
```

profile of v0, /device:TPU:2, one launch (start us, length us, event | category | flops | bytes accessed | tf_op | source)
XLA Modules:
  0.0 241.4 jit_solution(5547403851123938522)
XLA Ops:
  7.2 0.0 copy-start
  7.2 0.0 reduce-scatter.3.cloned.1.call-start
  7.2 1.6 copy-done
  8.8 5.1 %fusion.12 = f32[768,768]{1,0:T(8,128)} fusion(bf16[768,1536]{1,0:T(8,128)(2,1)S(1)} %copy-done, bf16[768,1536]{1,0:T(8,128)(2,1)} %param.9), kind=kOutput, calls=%fused_computation.21 | convolution fusion | flops 1811939328 | bytes 7077888 | tf_op jit(solution)/shard_map/dot_general | solution.py:25
  13.9 0.0 copy-start.1
  13.9 0.0 reduce-scatter.3.cloned.1.call-update
  13.9 0.0 all-gather.3.cloned.1.call-start
  14.0 46.3 %reduce-scatter.3.cloned.1.call-done = f32[96,768]{1,0:T(8,128)} async-done(((f32[768,768]{1,0:T(8,128)}), f32[96,768]{1,0:T(8,128)}) %reduce-scatter.3.cloned.1.call-update) | async-done | bytes 294928 | tf_op jit(solution)/shard_map/reduce_scatter | solution.py:24
  60.3 0.0 copy-done.1
  60.3 1.9 fusion.8
  62.1 0.0 all-gather.3.cloned.1.call-update
  62.2 0.0 all-gather.5.cloned.1.call-start
  62.2 0.7 all-gather.5.cloned.1.call-update
  62.9 0.0 reduce-scatter.5.cloned.1.call-start
  63.0 37.7 %all-gather.3.cloned.1.call-done = bf16[768,768]{1,0:T(8,128)(2,1)} async-done(((bf16[96,768]{1,0:T(8,128)(2,1)}), bf16[768,768]{1,0:T(8,128)(2,1)}) %all-gather.3.cloned.1.call-update) | async-done | bytes 1179664 | tf_op jit(solution)/shard_map/all_gather | solution.py:34
  100.7 6.2 %fusion.13 = f32[768,1536]{1,0:T(8,128)} fusion(bf16[768,768]{1,0:T(8,128)(2,1)} %all-gather.3.cloned.1.call-done, bf16[1536,768]{1,0:T(8,128)(2,1)} %param.8), kind=kOutput, calls=%fused_computation.22 | convolution fusion | flops 1811939328 | bytes 8257536 | tf_op jit(solution)/shard_map/dot_general | solution.py:46
  106.9 0.0 copy-start.2
  106.9 0.0 reduce-scatter.5.cloned.1.call-update
  106.9 1.2 copy-done.2
  108.1 5.1 %fusion = bf16[1536,768]{0,1:T(8,128)(2,1)} fusion(bf16[768,768]{1,0:T(8,128)(2,1)S(1)} %copy-done.2, bf16[768,1536]{1,0:T(8,128)(2,1)} %param.5), kind=kOutput, calls=%fused_computation.2 | convolution fusion | flops 1814298624 | bytes 5898240 | tf_op jit(solution)/shard_map/dot_general | solution.py:40
  113.2 4.3 %copy.8 = bf16[1536,768]{1,0:T(8,128)(2,1)} copy(bf16[1536,768]{0,1:T(8,128)(2,1)} %fusion) | data formatting | bytes 4718592
  117.5 22.2 %all-gather.5.cloned.1.call-done = bf16[768,768]{1,0:T(8,128)(2,1)} async-done(((bf16[96,768]{1,0:T(8,128)(2,1)}), bf16[768,768]{1,0:T(8,128)(2,1)}) %all-gather.5.cloned.1.call-update) | async-done | bytes 1179664 | tf_op jit(solution)/shard_map/all_gather | solution.py:33
  139.7 4.7 %multiply_convert_fusion = bf16[768,1536]{1,0:T(8,128)(2,1)} fusion(bf16[768,768]{1,0:T(8,128)(2,1)} %all-gather.5.cloned.1.call-done, bf16[768,1536]{1,0:T(8,128)(2,1)S(1)} %copy-done), kind=kOutput, calls=%fused_computation | convolution fusion | flops 1814298624 | bytes 5898240 | tf_op jit(solution)/shard_map/dot_general | solution.py:36
  144.4 88.9 %reduce-scatter.5.cloned.1.call-done = f32[24,1536]{1,0:T(8,128)} async-done(((f32[768,1536]{1,0:T(8,128)}), f32[24,1536]{1,0:T(8,128)}) %reduce-scatter.5.cloned.1.call-update) | async-done | bytes 147472 | tf_op jit(solution)/shard_map/reduce_scatter | solution.py:45
  233.3 1.6 convert_element_type.23
Async XLA Ops:
  7.2 1.7 copy-start
  7.2 53.1 %reduce-scatter.3.cloned.1.call-start = ((), (), s32[]{:S(2)}) async-start(), calls=%async_computation.2 | async-start | bytes 2654208 | tf_op jit(solution)/shard_map/reduce_scatter | solution.py:24
  13.9 46.3 %copy-start.1 = (bf16[96,768]{1,0:T(8,128)(2,1)S(1)}, bf16[96,768]{1,0:T(8,128)(2,1)}, u32[]{:S(2)}) copy-start(bf16[96,768]{1,0:T(8,128)(2,1)} %param.7) | copy-start | bytes 442372
  13.9 86.7 %all-gather.3.cloned.1.call-start = ((), (), s32[]{:S(2)}) async-start(), calls=%async_computation.3 | async-start | bytes 1327104 | tf_op jit(solution)/shard_map/all_gather | solution.py:34
  62.2 77.6 %all-gather.5.cloned.1.call-start = ((), (), s32[]{:S(2)}) async-start(), calls=%async_computation.5 | async-start | bytes 1327104 | tf_op jit(solution)/shard_map/all_gather | solution.py:33
  62.9 170.4 %reduce-scatter.5.cloned.1.call-start = ((), (), s32[]{:S(2)}) async-start(), calls=%async_computation.4 | async-start | bytes 4866048 | tf_op jit(solution)/shard_map/reduce_scatter | solution.py:45
  106.9 1.3 copy-start.2
Sparse Core Ops, SparseCore 0:
  14.1 46.1 reduce-scatter.2
  62.6 37.9 all-gather.2
  102.5 37.2 all-gather.4
  143.6 89.6 reduce-scatter.4
where the time goes:
time: 242 us; the launch traced here: 241 us
  waiting for transfers between devices  196 us (81%)
  matrix products  21.1 us (9%)
  between operations  13.8 us (6%)
  local copies, waits for them, and re-layouts  7.13 us (3%)
  other arithmetic  3.43 us (1%)
    reduce_scatter x1, waiting for transfers between devices, per_device(): lax.psum_scatter(lax.dot_general(block, w_in, (((1,), (1,)), ((), ())), p...  88.9 us
    reduce_scatter x1, waiting for transfers between devices, per_device(): lax.psum_scatter(lax.dot_general(block, w_out, (((1,), (1,)), ((), ())),...  46.3 us
    all_gather x1, waiting for transfers between devices, per_device(): lax.all_gather(hid_share, 'col', axis=0, tiled=True)  37.7 us
    all_gather x1, waiting for transfers between devices, per_device(): lax.all_gather(local_act.astype(jnp.bfloat16), 'col', axis=0, tiled=True)  22.2 us
    unnamed x7, local copies, waits for them, and re-layouts  7.13 us
    dot_general x1, matrix products, per_device(): lax.dot_general(block, w_in, (((1,), (1,)), ((), ())), preferred_element_...  6.2 us
    dot_general x1, matrix products, per_device(): lax.dot_general(inputs, hid_all, (((0,), (0,)), ((), ())), preferred_elem...  5.1 us
    dot_general x1, matrix products, per_device(): lax.dot_general(block, w_out, (((1,), (1,)), ((), ())), preferred_element...  5.09 us
  transfers between devices with their start and end apart: 4, of which 4 were waited for; matrix products, arithmetic and copies ran while one was open for 8% of the time, Pallas kernels for 0%

commit v1 on v0

--- a/solution.py
+++ b/solution.py
@@ -5,6 +5,24 @@
 from jax.sharding import PartitionSpec as P
 
 coef_c = math.sqrt(2.0 / math.pi)
+
+
+def collect(value, axis, dim):
+    ways, here, step = (lax.axis_size(axis), lax.axis_index(axis), value.shape[dim])
+    shape = [n * ways if d == dim else n for d, n in enumerate(value.shape)]
+    full = lax.dynamic_update_slice_in_dim(
+        jnp.zeros(shape, value.dtype), value, here * step, axis=dim
+    )
+    going_up = going_down = value
+    for far in range(1, ways // 2 + 1):
+        going_up = lax.ppermute(going_up, axis, [(d, (d + 1) % ways) for d in range(ways)])
+        full = lax.dynamic_update_slice_in_dim(full, going_up, (here - far) % ways * step, axis=dim)
+        if 2 * far < ways:
+            going_down = lax.ppermute(going_down, axis, [(d, (d - 1) % ways) for d in range(ways)])
+            full = lax.dynamic_update_slice_in_dim(
+                full, going_down, (here + far) % ways * step, axis=dim
+            )
+    return full
 
 
 def gelu_parts(pre_values):
@@ -31,7 +49,7 @@
     hid_share = (act_share * local_deriv).astype(jnp.bfloat16)
     activ_all, hid_all = (
         lax.all_gather(local_act.astype(jnp.bfloat16), "col", axis=0, tiled=True),
-        lax.all_gather(hid_share, "col", axis=0, tiled=True),
+        collect(hid_share, "col", 0),
     )
     grad_w_out = lax.dot_general(
         activ_all, out_grad, (((0,), (0,)), ((), ())), preferred_element_type=jnp.float32

time: 242 us -> 204 us (0.84)
  waiting for transfers between devices: 196 us -> 147 us
  starting transfers between devices: 0.16 us -> 10.1 us
  local copies, waits for them, and re-layouts: 7.13 us -> 9.61 us
    all_gather x1 -> x0, waiting for transfers between devices: 37.7 us -> none  [per_device(): lax.all_gather(hid_share, 'col', axis=0, tiled=True)]
    all_gather x1, waiting for transfers between devices: 22.2 us -> 0.26 us  [per_device(): lax.all_gather(local_act.astype(jnp.bfloat16), 'col', axis=0, tiled=True)]
    ppermute x0 -> x7, waiting for transfers between devices: none -> 20 us  [the longest x4 20 us: collect(): lax.ppermute(going_up, axis, [(d, (d + 1) % ways) for d in range(ways)])]
    ppermute x0 -> x7, starting transfers between devices: none -> 9.98 us  [the longest x3 9.15 us: collect(): lax.ppermute(going_down, axis, [(d, (d - 1) % ways) for d in range(ways)])]
    reduce_scatter x1, waiting for transfers between devices: 88.9 us -> 81.8 us  [per_device(): lax.psum_scatter(lax.dot_general(block, w_in, (((1,), (1,)), ((), ())), p...]
    unnamed x7 -> x9, local copies, waits for them, and re-layouts: 7.13 us -> 7.6 us
  transfers between devices with their start and end apart: 4 -> 10, of which waited for: 4 -> 7; matrix products, arithmetic and copies ran while one was open for 8% -> 11% of each run, Pallas kernels for 0% -> 0%
where the time goes in v1:
time: 204 us
  waiting for transfers between devices  147 us (72%)
  matrix products  19.2 us (9%)
  between operations  13.8 us (7%)
  starting transfers between devices  10.1 us (5%)
  local copies, waits for them, and re-layouts  9.61 us (5%)
  other arithmetic  4.09 us (2%)
    reduce_scatter x1, waiting for transfers between devices, per_device(): lax.psum_scatter(lax.dot_general(block, w_in, (((1,), (1,)), ((), ())), p...  81.8 us
    reduce_scatter x1, waiting for transfers between devices, per_device(): lax.psum_scatter(lax.dot_general(block, w_out, (((1,), (1,)), ((), ())),...  44.6 us
    ppermute x4, waiting for transfers between devices, collect(): lax.ppermute(going_up, axis, [(d, (d + 1) % ways) for d in range(ways)])  20 us
    ppermute x3, starting transfers between devices, collect(): lax.ppermute(going_down, axis, [(d, (d - 1) % ways) for d in range(ways)])  9.15 us
    unnamed x9, local copies, waits for them, and re-layouts  7.6 us
    dot_general x1, matrix products, per_device(): lax.dot_general(block, w_in, (((1,), (1,)), ((), ())), preferred_element_...  5.82 us
    dot_general x1, matrix products, per_device(): lax.dot_general(block, w_out, (((1,), (1,)), ((), ())), preferred_element...  5.09 us
    dot_general x1, matrix products, per_device(): lax.dot_general(activ_all, out_grad, (((0,), (0,)), ((), ())), preferred_...  4.85 us
  transfers between devices with their start and end apart: 10, of which 7 were waited for; matrix products, arithmetic and copies ran while one was open for 11% of the time, Pallas kernels for 0%

profile of v1, /device:TPU:2, one launch (start us, length us, event | category | flops | bytes accessed | tf_op | source)
XLA Modules:
  0.0 203.6 jit_solution(272559569247811881)
XLA Ops:
  7.2 0.0 copy-start
  7.2 0.0 reduce-scatter.3.cloned.1.call-start
  7.2 1.6 copy-done
  8.8 5.1 %fusion.13 = f32[768,768]{1,0:T(8,128)} fusion(bf16[768,1536]{1,0:T(8,128)(2,1)S(1)} %copy-done, bf16[768,1536]{1,0:T(8,128)(2,1)} %param.9), kind=kOutput, calls=%fused_computation.29 | convolution fusion | flops 1811939328 | bytes 7077888 | tf_op jit(solution)/shard_map/dot_general | solution.py:43
  13.9 0.0 copy-start.1
  13.9 0.0 reduce-scatter.3.cloned.1.call-update
  14.0 0.0 all-gather.2.cloned.1.call-start
  14.0 0.8 copy-done.1
  14.8 0.8 fusion.8
  15.6 0.0 all-gather.2.cloned.1.call-update
  15.6 0.0 reduce-scatter.5.cloned.1.call-start
  15.7 44.6 %reduce-scatter.3.cloned.1.call-done = f32[96,768]{1,0:T(8,128)} async-done(((f32[768,768]{1,0:T(8,128)}), f32[96,768]{1,0:T(8,128)}) %reduce-scatter.3.cloned.1.call-update) | async-done | bytes 294928 | tf_op jit(solution)/shard_map/reduce_scatter | solution.py:42
  60.3 0.0 copy-start.2
  60.3 0.1 broadcast_in_dim.3
  60.4 0.9 copy-done.2
  61.3 1.8 constant_dynamic-update-slice_fusion.7
  63.0 0.8 collective-permute-start
  63.9 2.4 %collective-permute-start.1 = (bf16[96,768]{1,0:T(8,128)(2,1)}, bf16[96,768]{1,0:T(8,128)(2,1)}, u32[]{:S(2)}, u32[]{:S(2)}) collective-permute-start(bf16[96,768]{1,0:T(8,128)(2,1)} %get-tuple-element.7), channel_id=1, source_target_pairs={{0,7},{1,0},{2,1},{3,2},{4,3},{5,4},{6,5},{7,6},{8,15},{9,8},{10,9... | collective-permute-start | bytes 442376 | tf_op jit(solution)/shard_map/ppermute | solution.py:21
  66.3 4.6 %collective-permute-done = bf16[96,768]{1,0:T(8,128)(2,1)} collective-permute-done((bf16[96,768]{1,0:T(8,128)(2,1)}, bf16[96,768]{1,0:T(8,128)(2,1)}, u32[]{:S(2)}, u32[]{:S(2)}) %collective-permute-start) | collective-permute-done | bytes 147488 | tf_op jit(solution)/shard_map/ppermute | solution.py:18
  70.9 0.0 collective-permute-start.2
  70.9 0.0 collective-permute-done.1
  70.9 3.5 %collective-permute-start.3 = (bf16[96,768]{1,0:T(8,128)(2,1)}, bf16[96,768]{1,0:T(8,128)(2,1)S(1)}, u32[]{:S(2)}, u32[]{:S(2)}) collective-permute-start(bf16[96,768]{1,0:T(8,128)(2,1)} %collective-permute-done.1), channel_id=1, source_target_pairs={{0,7},{1,0},{2,1},{3,2},{4,3},{5,4},{6,5},{7,6},{8,15},{9,8},{10,9... | collective-permute-start | bytes 442376 | tf_op jit(solution)/shard_map/ppermute | solution.py:21
  74.4 0.9 constant_dynamic-update-slice_fusion.6
  75.3 0.9 constant_dynamic-update-slice_fusion.5
  76.3 3.3 %collective-permute-done.2 = bf16[96,768]{1,0:T(8,128)(2,1)S(1)} collective-permute-done((bf16[96,768]{1,0:T(8,128)(2,1)}, bf16[96,768]{1,0:T(8,128)(2,1)S(1)}, u32[]{:S(2)}, u32[]{:S(2)}) %collective-permute-start.2) | collective-permute-done | bytes 147488 | tf_op jit(solution)/shard_map/ppermute | solution.py:18
  79.6 0.0 collective-permute-start.4
  79.6 0.0 collective-permute-done.3
  79.6 3.2 %collective-permute-start.5 = (bf16[96,768]{1,0:T(8,128)(2,1)S(1)}, bf16[96,768]{1,0:T(8,128)(2,1)S(1)}, u32[]{:S(2)}, u32[]{:S(2)}) collective-permute-start(bf16[96,768]{1,0:T(8,128)(2,1)S(1)} %collective-permute-done.3), channel_id=1, source_target_pairs={{0,7},{1,0},{2,1},{3,2},{4,3},{5,4},{6,5},{7,6},{8,15},{9,8},{10,9... | collective-permute-start | bytes 442376 | tf_op jit(solution)/shard_map/ppermute | solution.py:21
  82.9 4.5 %collective-permute-done.4 = bf16[96,768]{1,0:T(8,128)(2,1)S(1)} collective-permute-done((bf16[96,768]{1,0:T(8,128)(2,1)S(1)}, bf16[96,768]{1,0:T(8,128)(2,1)S(1)}, u32[]{:S(2)}, u32[]{:S(2)}) %collective-permute-start.4) | collective-permute-done | bytes 147488 | tf_op jit(solution)/shard_map/ppermute | solution.py:18
  87.4 0.0 collective-permute-start.6
  87.4 0.0 collective-permute-done.5
  87.5 7.5 %collective-permute-done.6 = bf16[96,768]{1,0:T(8,128)(2,1)S(1)} collective-permute-done((bf16[96,768]{1,0:T(8,128)(2,1)S(1)}, bf16[96,768]{1,0:T(8,128)(2,1)S(1)}, u32[]{:S(2)}, u32[]{:S(2)}) %collective-permute-start.6) | collective-permute-done | bytes 147488 | tf_op jit(solution)/shard_map/ppermute | solution.py:18
  95.0 5.8 %fusion.14 = f32[768,1536]{1,0:T(8,128)} fusion(bf16[768,768]{1,0:T(8,128)(2,1)S(1)} %constant_dynamic-update-slice_fusion, bf16[1536,768]{1,0:T(8,128)(2,1)} %param.8), kind=kOutput, calls=%fused_computation.30 | convolution fusion | flops 1811939328 | bytes 8257536 | tf_op jit(solution)/shard_map/dot_general | solution.py:64
  100.8 0.0 reduce-scatter.5.cloned.1.call-update
  100.8 0.3 all-gather.2.cloned.1.call-done
  101.1 0.0 copy-start.3
  101.1 4.9 %multiply_convert_fusion = bf16[768,1536]{1,0:T(8,128)(2,1)} fusion(bf16[768,768]{1,0:T(8,128)(2,1)} %all-gather.2.cloned.1.call-done, bf16[768,1536]{1,0:T(8,128)(2,1)S(1)} %copy-done), kind=kOutput, calls=%fused_computation | convolution fusion | flops 1814298624 | bytes 5898240 | tf_op jit(solution)/shard_map/dot_general | solution.py:54
  105.9 0.0 copy-done.3
  105.9 3.5 %fusion = bf16[1536,768]{0,1:T(8,128)(2,1)} fusion(bf16[768,768]{1,0:T(8,128)(2,1)S(1)} %constant_dynamic-update-slice_fusion, bf16[768,1536]{1,0:T(8,128)(2,1)S(1)} %copy-done.3), kind=kOutput, calls=%fused_computation.2 | convolution fusion | flops 1814298624 | bytes 5898240 | tf_op jit(solution)/shard_map/dot_general | solution.py:58
  109.4 4.3 %copy.8 = bf16[1536,768]{1,0:T(8,128)(2,1)} copy(bf16[1536,768]{0,1:T(8,128)(2,1)} %fusion) | data formatting | bytes 4718592
  113.7 81.8 %reduce-scatter.5.cloned.1.call-done = f32[24,1536]{1,0:T(8,128)} async-done(((f32[768,1536]{1,0:T(8,128)}), f32[24,1536]{1,0:T(8,128)}) %reduce-scatter.5.cloned.1.call-update) | async-done | bytes 147472 | tf_op jit(solution)/shard_map/reduce_scatter | solution.py:63
  195.5 1.6 convert_element_type.23
  (5 shorter events, 0.1 us)
Async XLA Ops:
  7.2 1.7 copy-start
  7.2 53.1 %reduce-scatter.3.cloned.1.call-start = ((), (), s32[]{:S(2)}) async-start(), calls=%async_computation.2 | async-start | bytes 2654208 | tf_op jit(solution)/shard_map/reduce_scatter | solution.py:42
  13.9 0.9 copy-start.1
  14.0 87.1 %all-gather.2.cloned.1.call-start = ((), (), s32[]{:S(2)}) async-start(), calls=%async_computation.4 | async-start | bytes 1327104 | tf_op jit(solution)/shard_map/all_gather | solution.py:51
  15.6 179.9 %reduce-scatter.5.cloned.1.call-start = ((), (), s32[]{:S(2)}) async-start(), calls=%async_computation.3 | async-start | bytes 4866048 | tf_op jit(solution)/shard_map/reduce_scatter | solution.py:63
  60.3 1.0 copy-start.2
  63.0 7.9 %collective-permute-start = (bf16[96,768]{1,0:T(8,128)(2,1)}, bf16[96,768]{1,0:T(8,128)(2,1)}, u32[]{:S(2)}, u32[]{:S(2)}) collective-permute-start(bf16[96,768]{1,0:T(8,128)(2,1)} %get-tuple-element.7), channel_id=1, source_target_pairs={{0,1},{1,2},{2,3},{3,4},{4,5},{5,6},{6,7},{7,0},{8,9},{9,10},{10,1... | collective-permute-start | bytes 442376 | tf_op jit(solution)/shard_map/ppermute | solution.py:18
  63.9 7.1 %collective-permute-start.1 = (bf16[96,768]{1,0:T(8,128)(2,1)}, bf16[96,768]{1,0:T(8,128)(2,1)}, u32[]{:S(2)}, u32[]{:S(2)}) collective-permute-start(bf16[96,768]{1,0:T(8,128)(2,1)} %get-tuple-element.7), channel_id=1, source_target_pairs={{0,7},{1,0},{2,1},{3,2},{4,3},{5,4},{6,5},{7,6},{8,15},{9,8},{10,9... | collective-permute-start | bytes 442376 | tf_op jit(solution)/shard_map/ppermute | solution.py:21
  70.9 8.7 %collective-permute-start.2 = (bf16[96,768]{1,0:T(8,128)(2,1)}, bf16[96,768]{1,0:T(8,128)(2,1)S(1)}, u32[]{:S(2)}, u32[]{:S(2)}) collective-permute-start(bf16[96,768]{1,0:T(8,128)(2,1)} %collective-permute-done), channel_id=1, source_target_pairs={{0,1},{1,2},{2,3},{3,4},{4,5},{5,6},{6,7},{7,0},{8,9},{9,10},{10,1... | collective-permute-start | bytes 442376 | tf_op jit(solution)/shard_map/ppermute | solution.py:18
  70.9 8.7 %collective-permute-start.3 = (bf16[96,768]{1,0:T(8,128)(2,1)}, bf16[96,768]{1,0:T(8,128)(2,1)S(1)}, u32[]{:S(2)}, u32[]{:S(2)}) collective-permute-start(bf16[96,768]{1,0:T(8,128)(2,1)} %collective-permute-done.1), channel_id=1, source_target_pairs={{0,7},{1,0},{2,1},{3,2},{4,3},{5,4},{6,5},{7,6},{8,15},{9,8},{10,9... | collective-permute-start | bytes 442376 | tf_op jit(solution)/shard_map/ppermute | solution.py:21
  79.6 7.8 %collective-permute-start.4 = (bf16[96,768]{1,0:T(8,128)(2,1)S(1)}, bf16[96,768]{1,0:T(8,128)(2,1)S(1)}, u32[]{:S(2)}, u32[]{:S(2)}) collective-permute-start(bf16[96,768]{1,0:T(8,128)(2,1)S(1)} %collective-permute-done.2), channel_id=1, source_target_pairs={{0,1},{1,2},{2,3},{3,4},{4,5},{5,6},{6,7},{7,0},{8,9},{9,10},{10,1... | collective-permute-start | bytes 442376 | tf_op jit(solution)/shard_map/ppermute | solution.py:18
  79.6 7.8 %collective-permute-start.5 = (bf16[96,768]{1,0:T(8,128)(2,1)S(1)}, bf16[96,768]{1,0:T(8,128)(2,1)S(1)}, u32[]{:S(2)}, u32[]{:S(2)}) collective-permute-start(bf16[96,768]{1,0:T(8,128)(2,1)S(1)} %collective-permute-done.3), channel_id=1, source_target_pairs={{0,7},{1,0},{2,1},{3,2},{4,3},{5,4},{6,5},{7,6},{8,15},{9,8},{10,9... | collective-permute-start | bytes 442376 | tf_op jit(solution)/shard_map/ppermute | solution.py:21
  87.4 7.6 %collective-permute-start.6 = (bf16[96,768]{1,0:T(8,128)(2,1)S(1)}, bf16[96,768]{1,0:T(8,128)(2,1)S(1)}, u32[]{:S(2)}, u32[]{:S(2)}) collective-permute-start(bf16[96,768]{1,0:T(8,128)(2,1)S(1)} %collective-permute-done.4), channel_id=1, source_target_pairs={{0,1},{1,2},{2,3},{3,4},{4,5},{5,6},{6,7},{7,0},{8,9},{9,10},{10,1... | collective-permute-start | bytes 442376 | tf_op jit(solution)/shard_map/ppermute | solution.py:18
  101.1 4.9 %copy-start.3 = (bf16[768,1536]{1,0:T(8,128)(2,1)S(1)}, bf16[768,1536]{1,0:T(8,128)(2,1)}, u32[]{:S(2)}) copy-start(bf16[768,1536]{1,0:T(8,128)(2,1)} %param.5) | copy-start | bytes 7077892
Sparse Core Ops, SparseCore 0:
  14.1 46.1 reduce-scatter.2
  62.7 38.3 all-gather.1
  105.1 90.3 reduce-scatter.4
